TPU v7x, 32 devices: a whole 2x2x4 slice. The times are simulated.
32 devices in a mesh: area: 4 (over y, core), pos: 8 (over z, x).
Axes of the slice: x: 2, y: 2, z: 4, core: 2. Of those that a mesh axis runs over, the one named last changes fastest.
Arguments:
- exit_wave: bfloat16 [128, 2, 128, 128], P(('area', 'pos')), may hold values from -6 to 6
- amplitude: bfloat16 [128, 128, 128], P(('area', 'pos')), may hold values from 0.19921875 to 5
- probe: float32 [2, 128, 128], replicated, may hold values from -4 to 4
- offsets: int32 [128, 2], P(('area', 'pos')), may hold values from 0 to 127
- owner: int32 [128, 1], P(('area', 'pos')), may hold values from 0 to 7; in each aligned block of 4 rows (0 to 3, 4 to 7, ...) at most 2 rows name the same one
Outputs:
- new_wave: bfloat16 [128, 2, 128, 128], P(('area', 'pos'))
- object_field: float32 [2, 512, 1024], P(None, 'area', 'pos')
Inputs may be any that keep to these rules, and one draw needn't show every extreme that they name: owner names the object tile column that holds the position's patch centre; of the 4 positions of one device at most 2 name the same tile.
All inputs are finite; a program needn't handle non-finite values.
Results may differ from a plain program's by a relative error of at most 0.0059.
Values may be sent and summed in bfloat16 or wider, within the bound.
No kernel may reach another device: no remote copies, remote signals or barrier semaphores. Data moves between devices by JAX's collectives and lax.ppermute only.
A program may use at most 64 MiB of HBM per device.

v0:
```python
import math
import jax
import jax.numpy as jnp
from jax import lax
from jax.sharding import PartitionSpec as P

F = 128
TS = 128
C = 2


def passed_along(value, axis, steps):
    count = lax.axis_size(axis)
    first, last = (max(0, -steps), min(count, count - steps))
    return lax.ppermute(value, axis, [(source, source + steps) for source in range(first, last)])


def extended(cells, sides, width):
    for axis, dim in sides:
        count = lax.axis_size(axis)
        ends = count - 1
        head = lax.slice_in_dim(cells, 0, width, axis=dim)
        tail = lax.slice_in_dim(cells, cells.shape[dim] - width, cells.shape[dim], axis=dim)
        cells = jnp.concatenate(
            [
                lax.ppermute(tail, axis, [(i, (i + 1) % count) for i in range(ends)]),
                cells,
                lax.ppermute(head, axis, [((i + 1) % count, i) for i in range(ends)]),
            ],
            axis=dim,
        )
    return cells


def fold_rows(canvas):
    margin = F // 2
    summed = canvas
    for step in (1, -1):
        edge = canvas[:, TS + margin :, :] if step == 1 else canvas[:, :margin, :]
        arrived = passed_along(edge, "area", step)
        first = margin if step == 1 else TS
        summed = summed.at[:, first : first + margin, :].add(arrived)
    return summed[:, margin : margin + TS, :]


def fold_columns(canvas):
    margin = F // 2
    summed = canvas
    for step in (1, -1):
        edge = canvas[:, :, TS + margin :] if step == 1 else canvas[:, :, :margin]
        arrived = passed_along(edge, "pos", step)
        first = margin if step == 1 else TS
        summed = summed.at[:, :, first : first + margin].add(arrived)
    return summed[:, :, margin : margin + TS]


def left_multiply(mat_re, mat_im, data_re, data_im):
    highest = lax.Precision.HIGHEST
    out_re = jnp.einsum("kn,bnm->bkm", mat_re, data_re, precision=highest) - jnp.einsum(
        "kn,bnm->bkm", mat_im, data_im, precision=highest
    )
    out_im = jnp.einsum("kn,bnm->bkm", mat_re, data_im, precision=highest) + jnp.einsum(
        "kn,bnm->bkm", mat_im, data_re, precision=highest
    )
    return (out_re, out_im)


def right_multiply(data_re, data_im, mat_re, mat_im):
    highest = lax.Precision.HIGHEST
    out_re = jnp.einsum("bkm,ml->bkl", data_re, mat_re, precision=highest) - jnp.einsum(
        "bkm,ml->bkl", data_im, mat_im, precision=highest
    )
    out_im = jnp.einsum("bkm,ml->bkl", data_re, mat_im, precision=highest) + jnp.einsum(
        "bkm,ml->bkl", data_im, mat_re, precision=highest
    )
    return (out_re, out_im)


def cut_patches(source, row_starts, col_starts):
    return jax.vmap(lambda r, c: lax.dynamic_slice(source, (jnp.int32(0), r, c), (2, F, F)))(
        row_starts, col_starts
    )


def weighted_waves(waves_bf, probe_re, probe_im):
    waves_f = waves_bf.astype(jnp.float32)
    first = probe_re * waves_f[:, 0] + probe_im * waves_f[:, 1]
    second = probe_re * waves_f[:, 1] - probe_im * waves_f[:, 0]
    return jnp.stack([first, second], 1).astype(jnp.bfloat16)


def accumulate(contrib, meta, power_map):
    live = meta[:, 2]
    ordering = jnp.argsort(1 - live, stable=True)
    live_count = jnp.sum(live)

    def add_one(number, canvas):
        chosen = ordering[number]
        piece = jnp.concatenate([contrib[chosen].astype(jnp.float32), power_map[None]], 0)
        where = (jnp.int32(0), meta[chosen, 0], meta[chosen, 1])
        old = lax.dynamic_slice(canvas, where, (3, F, F))
        return lax.dynamic_update_slice(canvas, old + piece, where)

    canvas = lax.fori_loop(0, live_count, add_one, jnp.zeros((3, TS + F, TS + F), jnp.float32))
    summed = fold_columns(fold_rows(canvas))
    return (summed[0:2] / (summed[2] + 0.1)[None], ordering, live_count)


def relaxed_update(waves_bf, amps_bf, patch_bf, probe_re, probe_im):
    pixel = jnp.arange(F, dtype=jnp.int32)
    product = pixel[:, None] * pixel[None, :] % F
    angle = product.astype(jnp.float32) * (2.0 * math.pi / F)
    scale_by = 1.0 / math.sqrt(F)
    twiddle_re = jnp.cos(angle) * scale_by
    twiddle_im = -jnp.sin(angle) * scale_by
    waves_f = waves_bf.astype(jnp.float32)
    patch_f = patch_bf.astype(jnp.float32)
    proj_re = probe_re * patch_f[:, 0] - probe_im * patch_f[:, 1]
    proj_im = probe_re * patch_f[:, 1] + probe_im * patch_f[:, 0]
    trial_re = 2.0 * proj_re - waves_f[:, 0]
    trial_im = 2.0 * proj_im - waves_f[:, 1]
    half_re, half_im = left_multiply(twiddle_re, twiddle_im, trial_re, trial_im)
    spectrum_re, spectrum_im = right_multiply(half_re, half_im, twiddle_re, twiddle_im)
    modulus = jnp.sqrt(spectrum_re * spectrum_re + spectrum_im * spectrum_im + 0.01)
    ratio = amps_bf.astype(jnp.float32) / modulus
    fitted_re = spectrum_re * ratio
    fitted_im = spectrum_im * ratio
    half_re, half_im = left_multiply(twiddle_re, -twiddle_im, fitted_re, fitted_im)
    back_re, back_im = right_multiply(half_re, half_im, twiddle_re, -twiddle_im)
    new_re = 0.75 * waves_f[:, 0] - 0.5 * proj_re + 0.75 * back_re
    new_im = 0.75 * waves_f[:, 1] - 0.5 * proj_im + 0.75 * back_im
    return jnp.stack([new_re, new_im], 1).astype(jnp.bfloat16)


def body(exit_wave, amplitude, probe, offsets, owner):
    margin = F // 2
    columns_count = lax.axis_size("pos")
    probe_re = probe[0]
    probe_im = probe[1]
    power_map = probe_re * probe_re + probe_im * probe_im
    target = owner[:, 0]
    one_hot = (target[:, None] == jnp.arange(columns_count, dtype=jnp.int32)[None, :]).astype(
        jnp.int32
    )
    rank_in = jnp.sum((jnp.cumsum(one_hot, axis=0) - 1) * one_hot, axis=1)
    slot_flat = target * C + rank_in
    slot_total = columns_count * C
    described = jnp.concatenate([offsets, jnp.ones((offsets.shape[0], 1), jnp.int32)], 1)
    send_meta = jnp.zeros((slot_total, 3), jnp.int32).at[slot_flat].set(described)
    contrib = weighted_waves(exit_wave, probe_re, probe_im)
    send_wave = jnp.zeros((slot_total, 2, F, F), jnp.bfloat16).at[slot_flat].set(contrib)
    got_wave, got_meta = (
        lax.all_to_all(send_wave, "pos", split_axis=0, concat_axis=0, tiled=True),
        lax.all_to_all(send_meta, "pos", split_axis=0, concat_axis=0, tiled=True),
    )
    object_tile, ordering, live_count = accumulate(got_wave, got_meta, power_map)
    object_half = object_tile.astype(jnp.bfloat16)
    strip = extended(object_half, (("area", 1),), margin)
    band_rows = lax.all_gather(strip, "pos", axis=2, tiled=True)
    band_rows = jnp.pad(band_rows, ((0, 0), (0, 0), (margin, margin)))
    own_patch = cut_patches(band_rows, offsets[:, 0], target * TS + offsets[:, 1])
    new_wave = relaxed_update(exit_wave, amplitude, own_patch, probe_re, probe_im)
    return (new_wave, object_tile)


def solution(mesh):
    return jax.shard_map(
        body,
        mesh=mesh,
        in_specs=(
            P(("area", "pos"), None, None, None),
            P(("area", "pos"), None, None),
            P(),
            P(("area", "pos"), None),
            P(("area", "pos"), None),
        ),
        out_specs=(P(("area", "pos"), None, None, None), P(None, "area", "pos")),
        check_vma=False,
    )
```

profile of v0, /device:TPU:0, one launch (start us, length us, event | category | flops | bytes accessed | tf_op | source)
XLA Modules:
  0.0 265.7 jit_solution(17552448648142886674)
XLA Ops:
  11.5 7.3 %all-to-all-start = ((s32[8,2,3]{2,1,0:T(2,128)}), s32[8,2,3]{2,1,0:T(2,128)S(1)}, u32[]{:S(2)}, u32[]{:S(2)}) async-start(s32[8,2,3]{2,1,0:T(2,128)} %bitcast.10), calls=%async_computation | async-start | bytes 16384 | tf_op jit(solution)/shard_map/all_to_all | solution.py:154
  22.0 2.2 scatter_fusion
  25.3 5.0 %all-to-all-start.1 = ((bf16[16,2,128,128]{3,2,1,0:T(8,128)(2,1)}), bf16[16,2,128,128]{3,2,1,0:T(8,128)(2,1)S(1)}, u32[]{:S(2)}, u32[]{:S(2)}) async-start(bf16[16,2,128,128]{3,2,1,0:T(8,128)(2,1)} %scatter_fusion), calls=%async_computation.1 | async-start | bytes 2097152 | tf_op jit(solution)/shard_map/all_to_all | solution.py:153
  32.3 23.4 %all-to-all-done.1 = bf16[16,2,128,128]{3,2,1,0:T(8,128)(2,1)S(1)} async-done(((bf16[16,2,128,128]{3,2,1,0:T(8,128)(2,1)}), bf16[16,2,128,128]{3,2,1,0:T(8,128)(2,1)S(1)}, u32[]{:S(2)}, u32[]{:S(2)}) %all-to-all-start.1) | async-done | bytes 1048608 | tf_op jit(solution)/shard_map/all_to_all | solution.py:153
  55.8 62.8 %while.15 = (s32[]{:T(128)}, f32[3,256,256]{2,1,0:T(8,128)S(1)}, s32[]{:T(128)}, s32[16]{0:T(128)S(1)}, s32[16,3]{0,1:T(4,128)S(1)}, /*index=5*/bf16[16,2,128,12...) while((s32[]{:T(128)}, f32[3,256,256]{2,1,0:T(8,128)S(1)}, ...), condition=%wide.region_7.8_spmd, body=%wide.region_6.7_spmd.sunk | while | flops 131086 | bytes 1179941 | solution.py:104
  63.3 2.8 %dynamic_update_slice.4 = f32[3,256,256]{2,1,0:T(8,128)S(1)} dynamic-update-slice(f32[3,256,256]{2,1,0:T(8,128)S(1)} %get-tuple-element.257, f32[3,128,128]{2,1,0:T(8,128)S(1)} %maximum_add_fusion.2, s32[]{:T(128)} %constant.154.clone.1..sunk, s32[]{:T(128)S(6)} %select_n.138, s32[]{:T(128)S(6)} %select_n.139) | dynamic-update-slice | bytes 393220 | tf_op jit(solution)/shard_map/while/body/dynamic_update_slice | solution.py:102
  73.5 2.9 %dynamic_update_slice.4 = f32[3,256,256]{2,1,0:T(8,128)S(1)} dynamic-update-slice(f32[3,256,256]{2,1,0:T(8,128)S(1)} %get-tuple-element.257, f32[3,128,128]{2,1,0:T(8,128)S(1)} %maximum_add_fusion.2, s32[]{:T(128)} %constant.154.clone.1..sunk, s32[]{:T(128)S(6)} %select_n.138, s32[]{:T(128)S(6)} %select_n.139) | dynamic-update-slice | bytes 393220 | tf_op jit(solution)/shard_map/while/body/dynamic_update_slice | solution.py:102
  83.9 2.9 %dynamic_update_slice.4 = f32[3,256,256]{2,1,0:T(8,128)S(1)} dynamic-update-slice(f32[3,256,256]{2,1,0:T(8,128)S(1)} %get-tuple-element.257, f32[3,128,128]{2,1,0:T(8,128)S(1)} %maximum_add_fusion.2, s32[]{:T(128)} %constant.154.clone.1..sunk, s32[]{:T(128)S(6)} %select_n.138, s32[]{:T(128)S(6)} %select_n.139) | dynamic-update-slice | bytes 393220 | tf_op jit(solution)/shard_map/while/body/dynamic_update_slice | solution.py:102
  94.3 2.8 %dynamic_update_slice.4 = f32[3,256,256]{2,1,0:T(8,128)S(1)} dynamic-update-slice(f32[3,256,256]{2,1,0:T(8,128)S(1)} %get-tuple-element.257, f32[3,128,128]{2,1,0:T(8,128)S(1)} %maximum_add_fusion.2, s32[]{:T(128)} %constant.154.clone.1..sunk, s32[]{:T(128)S(6)} %select_n.138, s32[]{:T(128)S(6)} %select_n.139) | dynamic-update-slice | bytes 393220 | tf_op jit(solution)/shard_map/while/body/dynamic_update_slice | solution.py:102
  104.5 3.0 %dynamic_update_slice.4 = f32[3,256,256]{2,1,0:T(8,128)S(1)} dynamic-update-slice(f32[3,256,256]{2,1,0:T(8,128)S(1)} %get-tuple-element.257, f32[3,128,128]{2,1,0:T(8,128)S(1)} %maximum_add_fusion.2, s32[]{:T(128)} %constant.154.clone.1..sunk, s32[]{:T(128)S(6)} %select_n.138, s32[]{:T(128)S(6)} %select_n.139) | dynamic-update-slice | bytes 393220 | tf_op jit(solution)/shard_map/while/body/dynamic_update_slice | solution.py:102
  115.0 2.9 %dynamic_update_slice.4 = f32[3,256,256]{2,1,0:T(8,128)S(1)} dynamic-update-slice(f32[3,256,256]{2,1,0:T(8,128)S(1)} %get-tuple-element.257, f32[3,128,128]{2,1,0:T(8,128)S(1)} %maximum_add_fusion.2, s32[]{:T(128)} %constant.154.clone.1..sunk, s32[]{:T(128)S(6)} %select_n.138, s32[]{:T(128)S(6)} %select_n.139) | dynamic-update-slice | bytes 393220 | tf_op jit(solution)/shard_map/while/body/dynamic_update_slice | solution.py:102
  122.3 2.0 collective-permute-done.1
  127.2 1.8 collective-permute-done.2
  129.1 1.3 scatter-add.16
  130.5 54.6 %collective-permute-done.3 = f32[3,128,64]{2,1,0:T(8,128)S(1)} collective-permute-done((f32[3,128,64]{2,1,0:T(8,128)S(1)}, f32[3,128,64]{2,1,0:T(8,128)S(1)}, u32[]{:S(2)}, u32[]{:S(2)}) %collective-permute-start.3) | collective-permute-done | bytes 98336 | tf_op jit(solution)/shard_map/ppermute | solution.py:15
  186.4 4.8 %collective-permute-start.4 = (bf16[2,64,128]{2,1,0:T(8,128)(2,1)S(1)}, bf16[2,64,128]{2,1,0:T(8,128)(2,1)S(1)}, u32[]{:S(2)}, u32[]{:S(2)}) collective-permute-start(bf16[2,64,128]{2,1,0:T(8,128)(2,1)S(1)} %get-tuple-element.161), channel_id=1, source_target_pairs={{0,8},{8,16},{16,24},{1,9},{9,17},{17,25},{2,10},{10,18},{18,26},{... | collective-permute-start | bytes 98312 | tf_op jit(solution)/shard_map/ppermute | solution.py:26
  192.5 2.3 collective-permute-done.5
  195.6 40.4 %all-gather.2.cloned.1.call-done = bf16[2,256,1024]{2,1,0:T(8,128)(2,1)} async-done(((bf16[2,256,128]{2,1,0:T(8,128)(2,1)}), bf16[2,256,1024]{2,1,0:T(8,128)(2,1)}) %all-gather.2.cloned.1.call-update) | async-done | bytes 1048592 | tf_op jit(solution)/shard_map/all_gather | solution.py:159
  236.0 1.9 pad.13
  237.9 8.0 %while.16 = (s32[]{:T(128)}, bf16[2,256,1152]{2,1,0:T(8,128)(2,1)S(1)}, s32[4,3]{1,0:T(4,128)S(1)}, bf16[4,2,128,128]{3,2,0,1:T(8,128)(2,1)S(1)}, s32[]{:T(128)}) while((s32[]{:T(128)}, bf16[2,256,1152]{2,1,0:T(8,128)(2,1)S(1)}, s32[4,3]{1,0:T(4,128)S(1)}, bf16[4,2,128,128]{3,2,0,1:T(8,128)(2,1)S(1)}, s32[]{:T(128)}) %tuple.76), condition=%wide.while_cond.4, body=%wide.while_body.4.sunk | while | flops 2 | bytes 131189 | solution.py:80
  238.5 1.3 bitcast_dynamic-update-slice_fusion.2
  240.5 1.3 bitcast_dynamic-update-slice_fusion.2
  242.4 1.3 bitcast_dynamic-update-slice_fusion.2
  244.3 1.3 bitcast_dynamic-update-slice_fusion.2
  (100 shorter events, 44.3 us)
Async XLA Ops:
  11.5 13.8 %all-to-all-start = ((s32[8,2,3]{2,1,0:T(2,128)}), s32[8,2,3]{2,1,0:T(2,128)S(1)}, u32[]{:S(2)}, u32[]{:S(2)}) async-start(s32[8,2,3]{2,1,0:T(2,128)} %bitcast.10), calls=%async_computation | async-start | bytes 16384 | tf_op jit(solution)/shard_map/all_to_all | solution.py:154
  24.2 6.2 %copy-start.1 = (f32[2,128,128]{2,1,0:T(8,128)S(1)}, f32[2,128,128]{2,1,0:T(8,128)}, u32[]{:S(2)}) copy-start(f32[2,128,128]{2,1,0:T(8,128)} %param.17) | copy-start | bytes 393220
  25.3 30.5 %all-to-all-start.1 = ((bf16[16,2,128,128]{3,2,1,0:T(8,128)(2,1)}), bf16[16,2,128,128]{3,2,1,0:T(8,128)(2,1)S(1)}, u32[]{:S(2)}, u32[]{:S(2)}) async-start(bf16[16,2,128,128]{3,2,1,0:T(8,128)(2,1)} %scatter_fusion), calls=%async_computation.1 | async-start | bytes 2097152 | tf_op jit(solution)/shard_map/all_to_all | solution.py:153
  30.3 205.7 %all-gather.2.cloned.1.call-start = ((), (), s32[]{:S(2)}) async-start(), calls=%async_computation.2 | async-start | bytes 1179648 | tf_op jit(solution)/shard_map/all_gather | solution.py:159
  118.6 2.4 collective-permute-start
  121.0 3.3 %collective-permute-start.1 = (f32[3,64,256]{2,1,0:T(8,128)S(1)}, f32[3,64,256]{2,1,0:T(8,128)S(1)}, u32[]{:S(2)}, u32[]{:S(2)}) collective-permute-start(f32[3,64,256]{2,1,0:T(8,128)S(1)} %get-tuple-element.153), channel_id=1, source_target_pairs={{8,0},{16,8},{24,16},{9,1},{17,9},{25,17},{10,2},{18,10},{26,18},{... | collective-permute-start | bytes 589832 | tf_op jit(solution)/shard_map/ppermute | solution.py:15
  124.5 4.5 %collective-permute-start.2 = (f32[3,128,64]{2,1,0:T(8,128)S(1)}, f32[3,128,64]{2,1,0:T(8,128)S(1)}, u32[]{:S(2)}, u32[]{:S(2)}) collective-permute-start(f32[3,128,64]{2,1,0:T(8,128)S(1)} %get-tuple-element.152), channel_id=1, source_target_pairs={{0,1},{1,2},{2,3},{3,4},{4,5},{5,6},{6,7},{8,9},{9,10},{10,11},{11... | collective-permute-start | bytes 294920 | tf_op jit(solution)/shard_map/ppermute | solution.py:15
  125.9 59.2 %collective-permute-start.3 = (f32[3,128,64]{2,1,0:T(8,128)S(1)}, f32[3,128,64]{2,1,0:T(8,128)S(1)}, u32[]{:S(2)}, u32[]{:S(2)}) collective-permute-start(f32[3,128,64]{2,1,0:T(8,128)S(1)} %get-tuple-element.151), channel_id=1, source_target_pairs={{1,0},{2,1},{3,2},{4,3},{5,4},{6,5},{7,6},{9,8},{10,9},{11,10},{12... | collective-permute-start | bytes 294920 | tf_op jit(solution)/shard_map/ppermute | solution.py:15
  186.4 6.1 %collective-permute-start.4 = (bf16[2,64,128]{2,1,0:T(8,128)(2,1)S(1)}, bf16[2,64,128]{2,1,0:T(8,128)(2,1)S(1)}, u32[]{:S(2)}, u32[]{:S(2)}) collective-permute-start(bf16[2,64,128]{2,1,0:T(8,128)(2,1)S(1)} %get-tuple-element.161), channel_id=1, source_target_pairs={{0,8},{8,16},{16,24},{1,9},{9,17},{17,25},{2,10},{10,18},{18,26},{... | collective-permute-start | bytes 98312 | tf_op jit(solution)/shard_map/ppermute | solution.py:26
  191.2 3.6 %collective-permute-start.5 = (bf16[2,64,128]{2,1,0:T(8,128)(2,1)S(1)}, bf16[2,64,128]{2,1,0:T(8,128)(2,1)S(1)}, u32[]{:S(2)}, u32[]{:S(2)}) collective-permute-start(bf16[2,64,128]{2,1,0:T(8,128)(2,1)S(1)} %get-tuple-element.162), channel_id=1, source_target_pairs={{8,0},{16,8},{24,16},{9,1},{17,9},{25,17},{10,2},{18,10},{26,18},{... | collective-permute-start | bytes 98312 | tf_op jit(solution)/shard_map/ppermute | solution.py:28
  249.7 2.2 copy-start
Sparse Core Ops, SparseCore 0:
  195.6 40.3 all-gather.1
where the time goes:
time: 267 us; the launch traced here: 266 us
  waiting for transfers between devices  127 us (48%)
  local copies, waits for them, and re-layouts  43.4 us (16%)
  loops' own time  37.5 us (14%)
  starting transfers between devices  23.6 us (9%)
  between operations  14.4 us (5%)
  matrix products  12 us (4%)
  other arithmetic  8.18 us (3%)
    ppermute x4, waiting for transfers between devices, passed_along(): lax.ppermute(value, axis, [(source, source + steps) for source in range(f...  59.5 us
    all_gather x1, waiting for transfers between devices, body(): band_rows = lax.all_gather(strip, 'pos', axis=2, tiled=True)  40.4 us
    another operation x1, loops' own time, accumulate(): lax.fori_loop(0, live_count, add_one, jnp.zeros((3, TS + F, TS + F), jnp....  37.2 us
    all_to_all x1, waiting for transfers between devices, body(): lax.all_to_all(send_wave, 'pos', split_axis=0, concat_axis=0, tiled=True)  23.4 us
    dynamic_update_slice x6, local copies, waits for them, and re-layouts, add_one(): return lax.dynamic_update_slice(canvas, old + piece, where)  17.2 us
    gather x12, local copies, waits for them, and re-layouts  7.71 us
    all_to_all x1, starting transfers between devices, body(): lax.all_to_all(send_meta, 'pos', split_axis=0, concat_axis=0, tiled=True)  7.28 us
  transfers between devices with their start and end apart: 9, of which 8 were waited for; matrix products, arithmetic and copies ran while one was open for 3% of the time, Pallas kernels for 0%

commit v1 on v0

--- a/solution.py
+++ b/solution.py
@@ -156,7 +156,12 @@
     object_tile, ordering, live_count = accumulate(got_wave, got_meta, power_map)
     object_half = object_tile.astype(jnp.bfloat16)
     strip = extended(object_half, (("area", 1),), margin)
-    band_rows = lax.all_gather(strip, "pos", axis=2, tiled=True)
+    ring = [strip]
+    for hop in range(7):
+        ring.append(lax.ppermute(ring[-1], "pos", [(dev, (dev + 1) % 8) for dev in range(8)]))
+    band_rows = jnp.roll(
+        jnp.concatenate(ring[::-1], axis=2), (lax.axis_index("pos") + 1) * ring[0].shape[2], axis=2
+    )
     band_rows = jnp.pad(band_rows, ((0, 0), (0, 0), (margin, margin)))
     own_patch = cut_patches(band_rows, offsets[:, 0], target * TS + offsets[:, 1])
     new_wave = relaxed_update(exit_wave, amplitude, own_patch, probe_re, probe_im)

time: 267 us -> 270 us (1.011)
  between operations: 14.4 us -> 1.13 us
  waiting for transfers between devices: 127 us -> 139 us
  starting transfers between devices: 23.6 us -> 26.7 us
    ppermute x0 -> x7, waiting for transfers between devices: none -> 52.1 us  [body(): lax.ppermute(ring[-1], 'pos', [(dev, (dev + 1) % 8) for dev in range(8)])]
    all_gather x1 -> x0, waiting for transfers between devices: 40.4 us -> none  [body(): band_rows = lax.all_gather(strip, 'pos', axis=2, tiled=True)]
    ppermute x0 -> x7, starting transfers between devices: none -> 3.19 us  [body(): lax.ppermute(ring[-1], 'pos', [(dev, (dev + 1) % 8) for dev in range(8)])]
  transfers between devices with their start and end apart: 9 -> 15, of which waited for: 8 -> 14; matrix products, arithmetic and copies ran while one was open for 3% -> 3% of each run, Pallas kernels for 0% -> 0%
where the time goes in v1:
time: 270 us; the launch traced here: 269 us
  waiting for transfers between devices  139 us (51%)
  local copies, waits for them, and re-layouts  43.8 us (16%)
  loops' own time  38.4 us (14%)
  starting transfers between devices  26.7 us (10%)
  matrix products  12 us (4%)
  other arithmetic  7.65 us (3%)
    ppermute x4, waiting for transfers between devices, passed_along(): lax.ppermute(value, axis, [(source, source + steps) for source in range(f...  60.6 us
    ppermute x7, waiting for transfers between devices, body(): lax.ppermute(ring[-1], 'pos', [(dev, (dev + 1) % 8) for dev in range(8)])  52.1 us
    another operation x1, loops' own time, accumulate(): lax.fori_loop(0, live_count, add_one, jnp.zeros((3, TS + F, TS + F), jnp....  38.1 us
    all_to_all x1, waiting for transfers between devices, body(): lax.all_to_all(send_wave, 'pos', split_axis=0, concat_axis=0, tiled=True)  23.4 us
    dynamic_update_slice x6, local copies, waits for them, and re-layouts, add_one(): return lax.dynamic_update_slice(canvas, old + piece, where)  17.2 us
    gather x12, local copies, waits for them, and re-layouts  8.16 us
    all_to_all x1, starting transfers between devices, body(): lax.all_to_all(send_meta, 'pos', split_axis=0, concat_axis=0, tiled=True)  7.28 us
  transfers between devices with their start and end apart: 15, of which 14 were waited for; matrix products, arithmetic and copies ran while one was open for 3% of the time, Pallas kernels for 0%

profile of v1, /device:TPU:0, one launch (start us, length us, event | category | flops | bytes accessed | tf_op | source)
XLA Modules:
  0.0 268.9 jit_solution(9863055999972811696)
XLA Ops:
  4.9 7.3 %all-to-all-start = ((s32[8,2,3]{2,1,0:T(2,128)}), s32[8,2,3]{2,1,0:T(2,128)S(1)}, u32[]{:S(2)}, u32[]{:S(2)}) async-start(s32[8,2,3]{2,1,0:T(2,128)} %bitcast.10), calls=%async_computation | async-start | bytes 16384 | tf_op jit(solution)/shard_map/all_to_all | solution.py:154
  15.4 2.2 scatter_fusion
  18.7 4.9 %all-to-all-start.1 = ((bf16[16,2,128,128]{3,2,1,0:T(8,128)(2,1)}), bf16[16,2,128,128]{3,2,1,0:T(8,128)(2,1)S(1)}, u32[]{:S(2)}, u32[]{:S(2)}) async-start(bf16[16,2,128,128]{3,2,1,0:T(8,128)(2,1)} %scatter_fusion), calls=%async_computation.1 | async-start | bytes 2097152 | tf_op jit(solution)/shard_map/all_to_all | solution.py:153
  25.7 23.4 %all-to-all-done.1 = bf16[16,2,128,128]{3,2,1,0:T(8,128)(2,1)S(1)} async-done(((bf16[16,2,128,128]{3,2,1,0:T(8,128)(2,1)}), bf16[16,2,128,128]{3,2,1,0:T(8,128)(2,1)S(1)}, u32[]{:S(2)}, u32[]{:S(2)}) %all-to-all-start.1) | async-done | bytes 1048608 | tf_op jit(solution)/shard_map/all_to_all | solution.py:153
  49.2 64.0 %while.15 = (s32[]{:T(128)}, f32[3,256,256]{2,1,0:T(8,128)S(1)}, s32[]{:T(128)}, s32[16]{0:T(128)S(1)}, s32[16,3]{0,1:T(4,128)S(1)}, /*index=5*/bf16[16,2,128,12...) while((s32[]{:T(128)}, f32[3,256,256]{2,1,0:T(8,128)S(1)}, ...), condition=%wide.region_7.8_spmd, body=%wide.region_6.7_spmd.sunk | while | flops 131086 | bytes 1179941 | solution.py:104
  56.8 2.8 %dynamic_update_slice.4 = f32[3,256,256]{2,1,0:T(8,128)S(1)} dynamic-update-slice(f32[3,256,256]{2,1,0:T(8,128)S(1)} %get-tuple-element.257, f32[3,128,128]{2,1,0:T(8,128)S(1)} %maximum_add_fusion.2, s32[]{:T(128)} %constant.176.clone.1..sunk, s32[]{:T(128)S(6)} %select_n.152, s32[]{:T(128)S(6)} %select_n.153) | dynamic-update-slice | bytes 393220 | tf_op jit(solution)/shard_map/while/body/dynamic_update_slice | solution.py:102
  67.3 2.9 %dynamic_update_slice.4 = f32[3,256,256]{2,1,0:T(8,128)S(1)} dynamic-update-slice(f32[3,256,256]{2,1,0:T(8,128)S(1)} %get-tuple-element.257, f32[3,128,128]{2,1,0:T(8,128)S(1)} %maximum_add_fusion.2, s32[]{:T(128)} %constant.176.clone.1..sunk, s32[]{:T(128)S(6)} %select_n.152, s32[]{:T(128)S(6)} %select_n.153) | dynamic-update-slice | bytes 393220 | tf_op jit(solution)/shard_map/while/body/dynamic_update_slice | solution.py:102
  77.9 2.9 %dynamic_update_slice.4 = f32[3,256,256]{2,1,0:T(8,128)S(1)} dynamic-update-slice(f32[3,256,256]{2,1,0:T(8,128)S(1)} %get-tuple-element.257, f32[3,128,128]{2,1,0:T(8,128)S(1)} %maximum_add_fusion.2, s32[]{:T(128)} %constant.176.clone.1..sunk, s32[]{:T(128)S(6)} %select_n.152, s32[]{:T(128)S(6)} %select_n.153) | dynamic-update-slice | bytes 393220 | tf_op jit(solution)/shard_map/while/body/dynamic_update_slice | solution.py:102
  88.5 2.8 %dynamic_update_slice.4 = f32[3,256,256]{2,1,0:T(8,128)S(1)} dynamic-update-slice(f32[3,256,256]{2,1,0:T(8,128)S(1)} %get-tuple-element.257, f32[3,128,128]{2,1,0:T(8,128)S(1)} %maximum_add_fusion.2, s32[]{:T(128)} %constant.176.clone.1..sunk, s32[]{:T(128)S(6)} %select_n.152, s32[]{:T(128)S(6)} %select_n.153) | dynamic-update-slice | bytes 393220 | tf_op jit(solution)/shard_map/while/body/dynamic_update_slice | solution.py:102
  99.0 3.0 %dynamic_update_slice.4 = f32[3,256,256]{2,1,0:T(8,128)S(1)} dynamic-update-slice(f32[3,256,256]{2,1,0:T(8,128)S(1)} %get-tuple-element.257, f32[3,128,128]{2,1,0:T(8,128)S(1)} %maximum_add_fusion.2, s32[]{:T(128)} %constant.176.clone.1..sunk, s32[]{:T(128)S(6)} %select_n.152, s32[]{:T(128)S(6)} %select_n.153) | dynamic-update-slice | bytes 393220 | tf_op jit(solution)/shard_map/while/body/dynamic_update_slice | solution.py:102
  109.7 2.9 %dynamic_update_slice.4 = f32[3,256,256]{2,1,0:T(8,128)S(1)} dynamic-update-slice(f32[3,256,256]{2,1,0:T(8,128)S(1)} %get-tuple-element.257, f32[3,128,128]{2,1,0:T(8,128)S(1)} %maximum_add_fusion.2, s32[]{:T(128)} %constant.176.clone.1..sunk, s32[]{:T(128)S(6)} %select_n.152, s32[]{:T(128)S(6)} %select_n.153) | dynamic-update-slice | bytes 393220 | tf_op jit(solution)/shard_map/while/body/dynamic_update_slice | solution.py:102
  116.9 2.0 collective-permute-done.1
  125.0 55.7 %collective-permute-done.3 = f32[3,128,64]{2,1,0:T(8,128)S(1)} collective-permute-done((f32[3,128,64]{2,1,0:T(8,128)S(1)}, f32[3,128,64]{2,1,0:T(8,128)S(1)}, u32[]{:S(2)}, u32[]{:S(2)}) %collective-permute-start.3) | collective-permute-done | bytes 98336 | tf_op jit(solution)/shard_map/ppermute | solution.py:15
  182.1 4.8 %collective-permute-start.4 = (bf16[2,64,128]{2,1,0:T(8,128)(2,1)S(1)}, bf16[2,64,128]{2,1,0:T(8,128)(2,1)S(1)}, u32[]{:S(2)}, u32[]{:S(2)}) collective-permute-start(bf16[2,64,128]{2,1,0:T(8,128)(2,1)S(1)} %get-tuple-element.161), channel_id=1, source_target_pairs={{0,8},{8,16},{16,24},{1,9},{9,17},{17,25},{2,10},{10,18},{18,26},{... | collective-permute-start | bytes 98312 | tf_op jit(solution)/shard_map/ppermute | solution.py:26
  188.2 2.3 collective-permute-done.5
  190.5 3.0 %collective-permute-start.6 = (bf16[2,256,128]{2,1,0:T(8,128)(2,1)S(1)}, bf16[2,256,128]{2,1,0:T(8,128)(2,1)S(1)}, u32[]{:S(2)}, u32[]{:S(2)}) collective-permute-start(bf16[2,256,128]{2,1,0:T(8,128)(2,1)S(1)} %pad_maximum_fusion.2), channel_id=1, source_target_pairs={{0,1},{1,2},{2,3},{3,4},{4,5},{5,6},{6,7},{7,0},{8,9},{9,10},{10,1... | collective-permute-start | bytes 393224 | tf_op jit(solution)/shard_map/ppermute | solution.py:161
  193.4 4.8 %collective-permute-done.6 = bf16[2,256,128]{2,1,0:T(8,128)(2,1)S(1)} collective-permute-done((bf16[2,256,128]{2,1,0:T(8,128)(2,1)S(1)}, bf16[2,256,128]{2,1,0:T(8,128)(2,1)S(1)}, u32[]{:S(2)}, u32[]{:S(2)}) %collective-permute-start.6) | collective-permute-done | bytes 131104 | tf_op jit(solution)/shard_map/ppermute | solution.py:161
  198.4 8.3 %collective-permute-done.7 = bf16[2,256,128]{2,1,0:T(8,128)(2,1)S(1)} collective-permute-done((bf16[2,256,128]{2,1,0:T(8,128)(2,1)S(1)}, bf16[2,256,128]{2,1,0:T(8,128)(2,1)S(1)}, u32[]{:S(2)}, u32[]{:S(2)}) %collective-permute-start.7) | collective-permute-done | bytes 131104 | tf_op jit(solution)/shard_map/ppermute | solution.py:161
  206.7 8.4 %collective-permute-done.8 = bf16[2,256,128]{2,1,0:T(8,128)(2,1)S(1)} collective-permute-done((bf16[2,256,128]{2,1,0:T(8,128)(2,1)S(1)}, bf16[2,256,128]{2,1,0:T(8,128)(2,1)S(1)}, u32[]{:S(2)}, u32[]{:S(2)}) %collective-permute-start.8) | collective-permute-done | bytes 131104 | tf_op jit(solution)/shard_map/ppermute | solution.py:161
  215.2 7.7 %collective-permute-done.9 = bf16[2,256,128]{2,1,0:T(8,128)(2,1)S(1)} collective-permute-done((bf16[2,256,128]{2,1,0:T(8,128)(2,1)S(1)}, bf16[2,256,128]{2,1,0:T(8,128)(2,1)S(1)}, u32[]{:S(2)}, u32[]{:S(2)}) %collective-permute-start.9) | collective-permute-done | bytes 131104 | tf_op jit(solution)/shard_map/ppermute | solution.py:161
  222.8 7.7 %collective-permute-done.10 = bf16[2,256,128]{2,1,0:T(8,128)(2,1)S(1)} collective-permute-done((bf16[2,256,128]{2,1,0:T(8,128)(2,1)S(1)}, bf16[2,256,128]{2,1,0:T(8,128)(2,1)S(1)}, u32[]{:S(2)}, u32[]{:S(2)}) %collective-permute-start.10) | collective-permute-done | bytes 131104 | tf_op jit(solution)/shard_map/ppermute | solution.py:161
  230.5 7.7 %collective-permute-done.11 = bf16[2,256,128]{2,1,0:T(8,128)(2,1)S(1)} collective-permute-done((bf16[2,256,128]{2,1,0:T(8,128)(2,1)S(1)}, bf16[2,256,128]{2,1,0:T(8,128)(2,1)S(1)}, u32[]{:S(2)}, u32[]{:S(2)}) %collective-permute-start.11) | collective-permute-done | bytes 131104 | tf_op jit(solution)/shard_map/ppermute | solution.py:161
  238.3 7.5 %collective-permute-done.12 = bf16[2,256,128]{2,1,0:T(8,128)(2,1)S(1)} collective-permute-done((bf16[2,256,128]{2,1,0:T(8,128)(2,1)S(1)}, bf16[2,256,128]{2,1,0:T(8,128)(2,1)S(1)}, u32[]{:S(2)}, u32[]{:S(2)}) %collective-permute-start.12) | collective-permute-done | bytes 131104 | tf_op jit(solution)/shard_map/ppermute | solution.py:161
  247.5 8.4 %while.16 = (s32[]{:T(128)}, bf16[2,256,1152]{2,1,0:T(8,128)(2,1)S(1)}, s32[4,3]{1,0:T(4,128)S(1)}, bf16[4,2,128,128]{3,2,0,1:T(8,128)(2,1)S(1)}, s32[]{:T(128)}) while((s32[]{:T(128)}, bf16[2,256,1152]{2,1,0:T(8,128)(2,1)S(1)}, s32[4,3]{1,0:T(4,128)S(1)}, bf16[4,2,128,128]{3,2,0,1:T(8,128)(2,1)S(1)}, s32[]{:T(128)}) %tuple.76), condition=%wide.while_cond.4, body=%wide.while_body.4.sunk | while | flops 2 | bytes 131189 | solution.py:80
  (128 shorter events, 54.6 us)
Async XLA Ops:
  4.9 13.8 %all-to-all-start = ((s32[8,2,3]{2,1,0:T(2,128)}), s32[8,2,3]{2,1,0:T(2,128)S(1)}, u32[]{:S(2)}, u32[]{:S(2)}) async-start(s32[8,2,3]{2,1,0:T(2,128)} %bitcast.10), calls=%async_computation | async-start | bytes 16384 | tf_op jit(solution)/shard_map/all_to_all | solution.py:154
  14.2 9.4 %copy-start.1 = (f32[2,128,128]{2,1,0:T(8,128)S(1)}, f32[2,128,128]{2,1,0:T(8,128)}, u32[]{:S(2)}) copy-start(f32[2,128,128]{2,1,0:T(8,128)} %param.17) | copy-start | bytes 393220
  18.7 30.4 %all-to-all-start.1 = ((bf16[16,2,128,128]{3,2,1,0:T(8,128)(2,1)}), bf16[16,2,128,128]{3,2,1,0:T(8,128)(2,1)S(1)}, u32[]{:S(2)}, u32[]{:S(2)}) async-start(bf16[16,2,128,128]{3,2,1,0:T(8,128)(2,1)} %scatter_fusion), calls=%async_computation.1 | async-start | bytes 2097152 | tf_op jit(solution)/shard_map/all_to_all | solution.py:153
  113.2 2.4 collective-permute-start
  115.6 3.3 %collective-permute-start.1 = (f32[3,64,256]{2,1,0:T(8,128)S(1)}, f32[3,64,256]{2,1,0:T(8,128)S(1)}, u32[]{:S(2)}, u32[]{:S(2)}) collective-permute-start(f32[3,64,256]{2,1,0:T(8,128)S(1)} %get-tuple-element.153), channel_id=1, source_target_pairs={{8,0},{16,8},{24,16},{9,1},{17,9},{25,17},{10,2},{18,10},{26,18},{... | collective-permute-start | bytes 589832 | tf_op jit(solution)/shard_map/ppermute | solution.py:15
  119.1 4.5 %collective-permute-start.2 = (f32[3,128,64]{2,1,0:T(8,128)S(1)}, f32[3,128,64]{2,1,0:T(8,128)S(1)}, u32[]{:S(2)}, u32[]{:S(2)}) collective-permute-start(f32[3,128,64]{2,1,0:T(8,128)S(1)} %get-tuple-element.152), channel_id=1, source_target_pairs={{0,1},{1,2},{2,3},{3,4},{4,5},{5,6},{6,7},{8,9},{9,10},{10,11},{11... | collective-permute-start | bytes 294920 | tf_op jit(solution)/shard_map/ppermute | solution.py:15
  120.5 60.2 %collective-permute-start.3 = (f32[3,128,64]{2,1,0:T(8,128)S(1)}, f32[3,128,64]{2,1,0:T(8,128)S(1)}, u32[]{:S(2)}, u32[]{:S(2)}) collective-permute-start(f32[3,128,64]{2,1,0:T(8,128)S(1)} %get-tuple-element.151), channel_id=1, source_target_pairs={{1,0},{2,1},{3,2},{4,3},{5,4},{6,5},{7,6},{9,8},{10,9},{11,10},{12... | collective-permute-start | bytes 294920 | tf_op jit(solution)/shard_map/ppermute | solution.py:15
  182.1 6.1 %collective-permute-start.4 = (bf16[2,64,128]{2,1,0:T(8,128)(2,1)S(1)}, bf16[2,64,128]{2,1,0:T(8,128)(2,1)S(1)}, u32[]{:S(2)}, u32[]{:S(2)}) collective-permute-start(bf16[2,64,128]{2,1,0:T(8,128)(2,1)S(1)} %get-tuple-element.161), channel_id=1, source_target_pairs={{0,8},{8,16},{16,24},{1,9},{9,17},{17,25},{2,10},{10,18},{18,26},{... | collective-permute-start | bytes 98312 | tf_op jit(solution)/shard_map/ppermute | solution.py:26
  186.8 3.6 %collective-permute-start.5 = (bf16[2,64,128]{2,1,0:T(8,128)(2,1)S(1)}, bf16[2,64,128]{2,1,0:T(8,128)(2,1)S(1)}, u32[]{:S(2)}, u32[]{:S(2)}) collective-permute-start(bf16[2,64,128]{2,1,0:T(8,128)(2,1)S(1)} %get-tuple-element.162), channel_id=1, source_target_pairs={{8,0},{16,8},{24,16},{9,1},{17,9},{25,17},{10,2},{18,10},{26,18},{... | collective-permute-start | bytes 98312 | tf_op jit(solution)/shard_map/ppermute | solution.py:28
  190.5 7.7 %collective-permute-start.6 = (bf16[2,256,128]{2,1,0:T(8,128)(2,1)S(1)}, bf16[2,256,128]{2,1,0:T(8,128)(2,1)S(1)}, u32[]{:S(2)}, u32[]{:S(2)}) collective-permute-start(bf16[2,256,128]{2,1,0:T(8,128)(2,1)S(1)} %pad_maximum_fusion.2), channel_id=1, source_target_pairs={{0,1},{1,2},{2,3},{3,4},{4,5},{5,6},{6,7},{7,0},{8,9},{9,10},{10,1... | collective-permute-start | bytes 393224 | tf_op jit(solution)/shard_map/ppermute | solution.py:161
  198.2 8.6 %collective-permute-start.7 = (bf16[2,256,128]{2,1,0:T(8,128)(2,1)S(1)}, bf16[2,256,128]{2,1,0:T(8,128)(2,1)S(1)}, u32[]{:S(2)}, u32[]{:S(2)}) collective-permute-start(bf16[2,256,128]{2,1,0:T(8,128)(2,1)S(1)} %collective-permute-done.6), channel_id=1, source_target_pairs={{0,1},{1,2},{2,3},{3,4},{4,5},{5,6},{6,7},{7,0},{8,9},{9,10},{10,1... | collective-permute-start | bytes 393224 | tf_op jit(solution)/shard_map/ppermute | solution.py:161
  206.7 8.4 %collective-permute-start.8 = (bf16[2,256,128]{2,1,0:T(8,128)(2,1)S(1)}, bf16[2,256,128]{2,1,0:T(8,128)(2,1)S(1)}, u32[]{:S(2)}, u32[]{:S(2)}) collective-permute-start(bf16[2,256,128]{2,1,0:T(8,128)(2,1)S(1)} %collective-permute-done.7), channel_id=1, source_target_pairs={{0,1},{1,2},{2,3},{3,4},{4,5},{5,6},{6,7},{7,0},{8,9},{9,10},{10,1... | collective-permute-start | bytes 393224 | tf_op jit(solution)/shard_map/ppermute | solution.py:161
  215.2 7.7 %collective-permute-start.9 = (bf16[2,256,128]{2,1,0:T(8,128)(2,1)S(1)}, bf16[2,256,128]{2,1,0:T(8,128)(2,1)S(1)}, u32[]{:S(2)}, u32[]{:S(2)}) collective-permute-start(bf16[2,256,128]{2,1,0:T(8,128)(2,1)S(1)} %collective-permute-done.8), channel_id=1, source_target_pairs={{0,1},{1,2},{2,3},{3,4},{4,5},{5,6},{6,7},{7,0},{8,9},{9,10},{10,1... | collective-permute-start | bytes 393224 | tf_op jit(solution)/shard_map/ppermute | solution.py:161
  222.8 7.7 %collective-permute-start.10 = (bf16[2,256,128]{2,1,0:T(8,128)(2,1)S(1)}, bf16[2,256,128]{2,1,0:T(8,128)(2,1)S(1)}, u32[]{:S(2)}, u32[]{:S(2)}) collective-permute-start(bf16[2,256,128]{2,1,0:T(8,128)(2,1)S(1)} %collective-permute-done.9), channel_id=1, source_target_pairs={{0,1},{1,2},{2,3},{3,4},{4,5},{5,6},{6,7},{7,0},{8,9},{9,10},{10,1... | collective-permute-start | bytes 393224 | tf_op jit(solution)/shard_map/ppermute | solution.py:161
  230.5 7.7 %collective-permute-start.11 = (bf16[2,256,128]{2,1,0:T(8,128)(2,1)S(1)}, bf16[2,256,128]{2,1,0:T(8,128)(2,1)S(1)}, u32[]{:S(2)}, u32[]{:S(2)}) collective-permute-start(bf16[2,256,128]{2,1,0:T(8,128)(2,1)S(1)} %collective-permute-done.10), channel_id=1, source_target_pairs={{0,1},{1,2},{2,3},{3,4},{4,5},{5,6},{6,7},{7,0},{8,9},{9,10},{10,1... | collective-permute-start | bytes 393224 | tf_op jit(solution)/shard_map/ppermute | solution.py:161
  238.2 7.7 %collective-permute-start.12 = (bf16[2,256,128]{2,1,0:T(8,128)(2,1)S(1)}, bf16[2,256,128]{2,1,0:T(8,128)(2,1)S(1)}, u32[]{:S(2)}, u32[]{:S(2)}) collective-permute-start(bf16[2,256,128]{2,1,0:T(8,128)(2,1)S(1)} %collective-permute-done.11), channel_id=1, source_target_pairs={{0,1},{1,2},{2,3},{3,4},{4,5},{5,6},{6,7},{7,0},{8,9},{9,10},{10,1... | collective-permute-start | bytes 393224 | tf_op jit(solution)/shard_map/ppermute | solution.py:161
  258.3 3.7 %copy-start = (bf16[4,128,128]{2,1,0:T(8,128)(2,1)S(1)}, bf16[4,128,128]{2,1,0:T(8,128)(2,1)}, u32[]{:S(2)}) copy-start(bf16[4,128,128]{2,1,0:T(8,128)(2,1)} %param.16) | copy-start | bytes 393220
